TPU v7x, 32 devices: a whole 2x2x4 slice. The times are simulated.
32 devices in a mesh: dp: 4 (over x, core), fsdp: 8 (over z, y).
Axes of the slice: x: 2, y: 2, z: 4, core: 2. Of those that a mesh axis runs over, the one named last changes fastest.
Arguments:
- byte_inputs: bfloat16 [3, 32, 1024, 768], P(None, ('dp', 'fsdp')), may hold values from -60 to 60
- lengths: int32 [3, 32], P(None, ('dp', 'fsdp')), may hold values from 256 to 1024, as said below
- latent_array: bfloat16 [256, 1280], P(None, ('dp', 'fsdp')), may hold values from -6 to 6
- gain_bytes: bfloat16 [768], P(('dp', 'fsdp')), may hold values from 0.25 to 1.75
- bias_bytes: bfloat16 [768], P(('dp', 'fsdp')), may hold values from -1.5 to 1.5
- gain_latent: bfloat16 [1280], P(('dp', 'fsdp')), may hold values from 0.25 to 1.75
- bias_latent: bfloat16 [1280], P(('dp', 'fsdp')), may hold values from -1.5 to 1.5
- query_weight: bfloat16 [1280, 256], P(('dp', 'fsdp')), may hold values from -0.15625 to 0.15625
- key_weight: bfloat16 [768, 256], P(('dp', 'fsdp')), may hold values from -0.21875 to 0.21875
- value_weight: bfloat16 [768, 1280], P(('dp', 'fsdp')), may hold values from -0.21875 to 0.21875
- output_weight: bfloat16 [1280, 1280], P(('dp', 'fsdp')), may hold values from -2.5 to 2.5
- gain_feed: bfloat16 [1280], P(('dp', 'fsdp')), may hold values from 0.25 to 1.75
- bias_feed: bfloat16 [1280], P(('dp', 'fsdp')), may hold values from -1.5 to 1.5
- up_weight: bfloat16 [1280, 1280], P(('dp', 'fsdp')), may hold values from -0.15625 to 0.15625
- down_weight: bfloat16 [1280, 1280], P(('dp', 'fsdp')), may hold values from -0.15625 to 0.15625
- cotangent: bfloat16 [3, 32, 256, 1280], P(None, ('dp', 'fsdp')), may hold values from -6 to 6
Outputs:
- latents_out: bfloat16 [3, 32, 256, 1280], P(None, ('dp', 'fsdp'))
- grad_inputs: bfloat16 [3, 32, 1024, 768], P(None, ('dp', 'fsdp'))
- grad_latent_array: float32 [256, 1280], P(None, ('dp', 'fsdp'))
- grad_gain_bytes: float32 [768], P(('dp', 'fsdp'))
- grad_bias_bytes: float32 [768], P(('dp', 'fsdp'))
- grad_gain_latent: float32 [1280], P(('dp', 'fsdp'))
- grad_bias_latent: float32 [1280], P(('dp', 'fsdp'))
- grad_query: float32 [1280, 256], P(('dp', 'fsdp'))
- grad_key: float32 [768, 256], P(('dp', 'fsdp'))
- grad_value: float32 [768, 1280], P(('dp', 'fsdp'))
- grad_output: float32 [1280, 1280], P(('dp', 'fsdp'))
- grad_gain_feed: float32 [1280], P(('dp', 'fsdp'))
- grad_bias_feed: float32 [1280], P(('dp', 'fsdp'))
- grad_up: float32 [1280, 1280], P(('dp', 'fsdp'))
- grad_down: float32 [1280, 1280], P(('dp', 'fsdp'))
Inputs may be any that keep to these rules, and one draw needn't show every extreme that they name: `lengths`: slots at or past a sequence's length are padding; in every micro-batch some sequence fills all 1024 slots.
All inputs are finite; a program needn't handle non-finite values.
Results may differ from a plain program's by a relative error of at most 0.012.
The roundings to bfloat16 on the way count: a program that leaves them out, or rounds other values in their place, can miss the bound.
Values may be sent and summed in bfloat16 or wider, within the bound.
No kernel may reach another device: no remote copies, remote signals or barrier semaphores. Data moves between devices by JAX's collectives and lax.ppermute only.
A program may use at most 192 MiB of HBM per device.

v0:
```python
import jax
import jax.numpy as jnp
from jax import lax
from jax.sharding import PartitionSpec as P

NL = 256
QK = 256
V = 1280
HEADS = 8
MB = 3
epsilon = 1e-05


def normalize(source, gain_vector, bias_vector):
    average = jnp.mean(source, axis=-1, keepdims=True)
    centered = source - average
    variance = jnp.mean(centered * centered, axis=-1, keepdims=True)
    return centered * lax.rsqrt(variance + epsilon) * gain_vector + bias_vector


def gelu_exact(upper_rows):
    return jax.nn.gelu(upper_rows, approximate=False)


def outer_sum(left_side, right_side):
    return jnp.einsum("rd,rf->df", left_side, right_side, preferred_element_type=jnp.float32)


def back_dot(left_side, right_side):
    return jnp.einsum("rf,df->rd", left_side, right_side, preferred_element_type=jnp.float32)


def attention_scores(query_heads, key_heads, length, factor):
    scores = (
        jnp.einsum("nhd,shd->hns", query_heads, key_heads, preferred_element_type=jnp.float32)
        * factor
    )
    live_mask = lax.iota(jnp.int32, key_heads.shape[0]) < length
    return jnp.where(live_mask[None, None, :], scores, -1e30)


def per_device(
    byte_inputs,
    lengths,
    latent_array,
    gain_bytes,
    bias_bytes,
    gain_latent,
    bias_latent,
    query_weight,
    key_weight,
    value_weight,
    output_weight,
    gain_feed,
    bias_feed,
    up_weight,
    down_weight,
    cotangent,
):
    query_width = QK // HEADS
    value_width = V // HEADS
    factor = query_width ** (-0.5)
    outputs = []
    input_grads = []
    summed = None
    owned_sums = None
    for micro_index in range(MB):
        gathered = (
            lax.all_gather(latent_array, ("dp", "fsdp"), axis=1, tiled=True),
            lax.all_gather(gain_bytes, ("dp", "fsdp"), axis=0, tiled=True),
            lax.all_gather(bias_bytes, ("dp", "fsdp"), axis=0, tiled=True),
            lax.all_gather(gain_latent, ("dp", "fsdp"), axis=0, tiled=True),
            lax.all_gather(bias_latent, ("dp", "fsdp"), axis=0, tiled=True),
            lax.all_gather(query_weight, ("dp", "fsdp"), axis=0, tiled=True),
            lax.all_gather(key_weight, ("dp", "fsdp"), axis=0, tiled=True),
            lax.all_gather(value_weight, ("dp", "fsdp"), axis=0, tiled=True),
            lax.all_gather(output_weight, ("dp", "fsdp"), axis=0, tiled=True),
            lax.all_gather(gain_feed, ("dp", "fsdp"), axis=0, tiled=True),
            lax.all_gather(bias_feed, ("dp", "fsdp"), axis=0, tiled=True),
            lax.all_gather(up_weight, ("dp", "fsdp"), axis=0, tiled=True),
            lax.all_gather(down_weight, ("dp", "fsdp"), axis=0, tiled=True),
        )
        (
            full_latent,
            full_gain_bytes,
            full_bias_bytes,
            full_gain_latent,
            full_bias_latent,
            full_query,
            full_key,
            full_value,
            full_output,
            full_gain_feed,
            full_bias_feed,
            full_up,
            full_down,
        ) = gathered
        inputs = byte_inputs[micro_index, 0].astype(jnp.float32)
        length = lengths[micro_index, 0]
        normed_bytes, pull_bytes = jax.vjp(
            normalize,
            inputs,
            full_gain_bytes.astype(jnp.float32),
            full_bias_bytes.astype(jnp.float32),
        )
        bytes_low = normed_bytes.astype(jnp.bfloat16)
        key_rows = jnp.dot(bytes_low, full_key, preferred_element_type=jnp.float32).astype(
            jnp.bfloat16
        )
        value_rows = jnp.dot(bytes_low, full_value, preferred_element_type=jnp.float32).astype(
            jnp.bfloat16
        )
        latent_float = full_latent.astype(jnp.float32)
        normed_latent, pull_latent = jax.vjp(
            normalize,
            latent_float,
            full_gain_latent.astype(jnp.float32),
            full_bias_latent.astype(jnp.float32),
        )
        latent_low = normed_latent.astype(jnp.bfloat16)
        queries = jnp.dot(latent_low, full_query, preferred_element_type=jnp.float32).astype(
            jnp.bfloat16
        )
        query_heads = queries.reshape(NL, HEADS, query_width)
        key_heads = key_rows.reshape(-1, HEADS, query_width)
        value_heads = value_rows.reshape(-1, HEADS, value_width)
        scores = attention_scores(query_heads, key_heads, length, factor)
        top_score = jnp.max(scores, axis=-1, keepdims=True)
        logsum = top_score[:, :, 0] + jnp.log(jnp.sum(jnp.exp(scores - top_score), axis=-1))
        probability = jnp.exp(scores - logsum[:, :, None])
        mixed_rows = (
            jnp.einsum(
                "hns,shd->nhd",
                probability.astype(jnp.bfloat16),
                value_heads,
                preferred_element_type=jnp.float32,
            )
            .reshape(NL, V)
            .astype(jnp.bfloat16)
        )
        first_sum = latent_float + jnp.dot(
            mixed_rows, full_output, preferred_element_type=jnp.float32
        )
        normed_middle, pull_middle = jax.vjp(
            normalize,
            first_sum,
            full_gain_feed.astype(jnp.float32),
            full_bias_feed.astype(jnp.float32),
        )
        middle_low = normed_middle.astype(jnp.bfloat16)
        upper_rows = jnp.dot(middle_low, full_up, preferred_element_type=jnp.float32)
        hidden_float, pull_gelu = jax.vjp(gelu_exact, upper_rows)
        hidden = hidden_float.astype(jnp.bfloat16)
        result = first_sum + jnp.dot(hidden, full_down, preferred_element_type=jnp.float32)
        outputs.append(result.astype(jnp.bfloat16))
        gathered = (
            lax.all_gather(latent_array, ("dp", "fsdp"), axis=1, tiled=True),
            lax.all_gather(gain_bytes, ("dp", "fsdp"), axis=0, tiled=True),
            lax.all_gather(bias_bytes, ("dp", "fsdp"), axis=0, tiled=True),
            lax.all_gather(gain_latent, ("dp", "fsdp"), axis=0, tiled=True),
            lax.all_gather(bias_latent, ("dp", "fsdp"), axis=0, tiled=True),
            lax.all_gather(query_weight, ("dp", "fsdp"), axis=0, tiled=True),
            lax.all_gather(key_weight, ("dp", "fsdp"), axis=0, tiled=True),
            lax.all_gather(value_weight, ("dp", "fsdp"), axis=0, tiled=True),
            lax.all_gather(output_weight, ("dp", "fsdp"), axis=0, tiled=True),
            lax.all_gather(gain_feed, ("dp", "fsdp"), axis=0, tiled=True),
            lax.all_gather(bias_feed, ("dp", "fsdp"), axis=0, tiled=True),
            lax.all_gather(up_weight, ("dp", "fsdp"), axis=0, tiled=True),
            lax.all_gather(down_weight, ("dp", "fsdp"), axis=0, tiled=True),
        )
        (
            full_latent,
            full_gain_bytes,
            full_bias_bytes,
            full_gain_latent,
            full_bias_latent,
            full_query,
            full_key,
            full_value,
            full_output,
            full_gain_feed,
            full_bias_feed,
            full_up,
            full_down,
        ) = gathered
        cotangent_row = cotangent[micro_index, 0].astype(jnp.float32)
        down_low = cotangent_row.astype(jnp.bfloat16)
        grad_down = outer_sum(hidden, down_low)
        (upper_grad,) = pull_gelu(back_dot(down_low, full_down))
        upper_low = upper_grad.astype(jnp.bfloat16)
        grad_up = outer_sum(middle_low, upper_low)
        first_extra, grad_gain_feed, grad_bias_feed = pull_middle(back_dot(upper_low, full_up))
        first_grad = cotangent_row + first_extra
        attend_low = first_grad.astype(jnp.bfloat16)
        grad_output = outer_sum(mixed_rows, attend_low)
        mixed_grad = (
            back_dot(attend_low, full_output).astype(jnp.bfloat16).reshape(NL, HEADS, value_width)
        )
        scores = attention_scores(query_heads, key_heads, length, factor)
        probability = jnp.exp(scores - logsum[:, :, None])
        weight_grad = jnp.einsum(
            "nhd,shd->hns", mixed_grad, value_heads, preferred_element_type=jnp.float32
        )
        value_grad = (
            jnp.einsum(
                "hns,nhd->shd",
                probability.astype(jnp.bfloat16),
                mixed_grad,
                preferred_element_type=jnp.float32,
            )
            .reshape(-1, V)
            .astype(jnp.bfloat16)
        )
        score_grad = probability * (
            weight_grad - jnp.sum(weight_grad * probability, axis=-1, keepdims=True)
        )
        score_low = score_grad.astype(jnp.bfloat16)
        query_grad = (
            (
                jnp.einsum("hns,shd->nhd", score_low, key_heads, preferred_element_type=jnp.float32)
                * factor
            )
            .reshape(NL, QK)
            .astype(jnp.bfloat16)
        )
        key_grad = (
            (
                jnp.einsum(
                    "hns,nhd->shd", score_low, query_heads, preferred_element_type=jnp.float32
                )
                * factor
            )
            .reshape(-1, QK)
            .astype(jnp.bfloat16)
        )
        grad_query = outer_sum(latent_low, query_grad)
        latent_extra, grad_gain_latent, grad_bias_latent = pull_latent(
            back_dot(query_grad, full_query)
        )
        grad_latent = first_grad + latent_extra
        grad_key = outer_sum(bytes_low, key_grad)
        grad_value = outer_sum(bytes_low, value_grad)
        source_grad = back_dot(key_grad, full_key) + back_dot(value_grad, full_value)
        input_extra, grad_gain_bytes, grad_bias_bytes = pull_bytes(source_grad)
        input_grads.append(input_extra.astype(jnp.bfloat16))
        local_grads = (
            grad_latent,
            grad_gain_bytes,
            grad_bias_bytes,
            grad_gain_latent,
            grad_bias_latent,
            grad_query,
            grad_key,
            grad_value,
            grad_output,
            grad_gain_feed,
            grad_bias_feed,
            grad_up,
            grad_down,
        )
        summed = local_grads if summed is None else jax.tree.map(jnp.add, summed, local_grads)
    (
        sum_latent,
        sum_gain_bytes,
        sum_bias_bytes,
        sum_gain_latent,
        sum_bias_latent,
        sum_query,
        sum_key,
        sum_value,
        sum_output,
        sum_gain_feed,
        sum_bias_feed,
        sum_up,
        sum_down,
    ) = summed
    owned_sums = (
        lax.psum_scatter(sum_latent, ("dp", "fsdp"), scatter_dimension=1, tiled=True),
        lax.psum_scatter(sum_gain_bytes, ("dp", "fsdp"), scatter_dimension=0, tiled=True),
        lax.psum_scatter(sum_bias_bytes, ("dp", "fsdp"), scatter_dimension=0, tiled=True),
        lax.psum_scatter(sum_gain_latent, ("dp", "fsdp"), scatter_dimension=0, tiled=True),
        lax.psum_scatter(sum_bias_latent, ("dp", "fsdp"), scatter_dimension=0, tiled=True),
        lax.psum_scatter(sum_query, ("dp", "fsdp"), scatter_dimension=0, tiled=True),
        lax.psum_scatter(sum_key, ("dp", "fsdp"), scatter_dimension=0, tiled=True),
        lax.psum_scatter(sum_value, ("dp", "fsdp"), scatter_dimension=0, tiled=True),
        lax.psum_scatter(sum_output, ("dp", "fsdp"), scatter_dimension=0, tiled=True),
        lax.psum_scatter(sum_gain_feed, ("dp", "fsdp"), scatter_dimension=0, tiled=True),
        lax.psum_scatter(sum_bias_feed, ("dp", "fsdp"), scatter_dimension=0, tiled=True),
        lax.psum_scatter(sum_up, ("dp", "fsdp"), scatter_dimension=0, tiled=True),
        lax.psum_scatter(sum_down, ("dp", "fsdp"), scatter_dimension=0, tiled=True),
    )
    latents_out = jnp.stack(outputs)[:, None]
    grad_inputs = jnp.stack(input_grads)[:, None]
    return (latents_out, grad_inputs) + tuple(owned_sums)


def solution(mesh):
    return jax.shard_map(
        per_device,
        mesh=mesh,
        in_specs=(
            P(None, ("dp", "fsdp"), None, None),
            P(None, ("dp", "fsdp")),
            P(None, ("dp", "fsdp")),
            P(("dp", "fsdp")),
            P(("dp", "fsdp")),
            P(("dp", "fsdp")),
            P(("dp", "fsdp")),
            P(("dp", "fsdp"), None),
            P(("dp", "fsdp"), None),
            P(("dp", "fsdp"), None),
            P(("dp", "fsdp"), None),
            P(("dp", "fsdp")),
            P(("dp", "fsdp")),
            P(("dp", "fsdp"), None),
            P(("dp", "fsdp"), None),
            P(None, ("dp", "fsdp"), None, None),
        ),
        out_specs=(
            P(None, ("dp", "fsdp"), None, None),
            P(None, ("dp", "fsdp"), None, None),
            P(None, ("dp", "fsdp")),
            P(("dp", "fsdp")),
            P(("dp", "fsdp")),
            P(("dp", "fsdp")),
            P(("dp", "fsdp")),
            P(("dp", "fsdp"), None),
            P(("dp", "fsdp"), None),
            P(("dp", "fsdp"), None),
            P(("dp", "fsdp"), None),
            P(("dp", "fsdp")),
            P(("dp", "fsdp")),
            P(("dp", "fsdp"), None),
            P(("dp", "fsdp"), None),
        ),
        check_vma=False,
    )
```

profile of v0, /device:TPU:0, one launch (start us, length us, event | category | flops | bytes accessed | tf_op | source)
XLA Modules:
  0.0 1375.6 jit_solution(13956663669413720624)
XLA Ops:
  10.1 74.3 %all_gather.26 = bf16[256,1280]{0,1:T(8,128)(2,1)S(1)} all-gather(bf16[256,40]{0,1:T(8,128)(2,1)} %param.18), channel_id=1, replica_groups=mesh['dp'=4,'fsdp'=8] {'dp','fsdp'}, dimensions={1}, use_global_device_ids=true | all-gather | bytes 675840 | tf_op jit(solution)/shard_map/all_gather | solution.py:69
  86.7 37.7 %all-reduce.13 = (bf16[768]{0:T(1024)(128)(2,1)S(1)}, bf16[768]{0:T(1024)(128)(2,1)S(1)}, bf16[1280]{0:T(1024)(128)(2,1)S(1)}, bf16[1280]{0:T(1024)(128)(2,1)S(1...) all-reduce(bf16[768]{0:T(1024)(128)(2,1)S(1)} %dynamic-update-slice, ...), channel_id=1, replica_groups=mesh['dp'=4,'fsdp'=8] {'dp','fsdp'}, use_global_device_ids=true, to_apply=%add.1 | all-reduce | flops 6656 | bytes 26624
  124.4 71.7 %all_gather.32 = bf16[1280,256]{1,0:T(8,128)(2,1)S(1)} all-gather(bf16[40,256]{1,0:T(8,128)(2,1)S(1)} %copy-done.117), channel_id=1, replica_groups=mesh['dp'=4,'fsdp'=8] {'dp','fsdp'}, dimensions={0}, use_global_device_ids=true | all-gather | bytes 675840 | tf_op jit(solution)/shard_map/all_gather | solution.py:74
  202.2 66.3 %all_gather.33 = bf16[768,256]{1,0:T(8,128)(2,1)S(1)} all-gather(bf16[24,256]{1,0:T(8,128)(2,1)S(1)} %copy-done.144), channel_id=1, replica_groups=mesh['dp'=4,'fsdp'=8] {'dp','fsdp'}, dimensions={0}, use_global_device_ids=true | all-gather | bytes 405504 | tf_op jit(solution)/shard_map/all_gather | solution.py:75
  289.5 4.5 convolution_convert_fusion.2
  296.9 4.5 convolution_convert_fusion.1
  304.2 6.0 convolution_convert_fusion
  313.2 8.1 convolution_convert_fusion.11
  321.3 6.5 convolution_convert_fusion.10
  339.0 7.0 multiply_convert_fusion.5
  346.0 4.9 multiply_convert_fusion.4
  351.0 5.1 multiply_convert_fusion.3
  356.1 4.0 add_convert_fusion.4
  380.2 6.8 multiply_reduce_fusion.2
  397.4 6.7 multiply_reduce_fusion.1
  414.8 6.7 multiply_reduce_fusion
  440.7 4.8 add_add_fusion.10
  448.4 7.2 convolution_convert_fusion.8
  455.7 7.2 convolution_convert_fusion.7
  463.2 5.1 fusion.179
  475.1 4.6 add_add_fusion.3
  484.0 3.9 convolution_add_fusion.2
  504.5 4.1 fusion.204
  516.9 7.2 fusion.47
  524.3 39.1 %all-reduce.12 = (f32[768]{0:T(1024)S(1)}, f32[768]{0:T(1024)S(1)}, f32[1280]{0:T(1024)S(1)}, f32[1280]{0:T(1024)S(1)}, f32[1280]{0:T(1024)S(1)}, /*index=5*/f32[1280]{0:T(1024)S(1)}) all-reduce(f32[768]{0:T(1024)S(1)} %add_add_fusion.19, f32[768]{0:T(1024)S(1)} %add_add_fusion.18, ...), channel_id=3, replica_groups=mesh['dp'=4,'fsdp'=8] {'dp','fsdp'}, use_global_device_ids=true, to_apply=%region_45.46.clone | all-reduce | flops 6656 | bytes 53248
  567.0 7.6 fusion.191
  583.4 79.2 %reduce-scatter.10.cloned.1.call-done = f32[40,256]{1,0:T(8,128)} async-done(((f32[1280,256]{1,0:T(8,128)}), f32[40,256]{1,0:T(8,128)}) %reduce-scatter.10.cloned.1.call-update) | async-done | bytes 40976 | tf_op jit(solution)/shard_map/reduce_scatter | solution.py:283
  662.6 135.4 %reduce-scatter.22.cloned.1.call-done = f32[40,256]{1,0:T(8,128)} async-done(((f32[1280,256]{1,0:T(8,128)}), f32[40,256]{1,0:T(8,128)}) %reduce-scatter.22.cloned.1.call-update) | async-done | bytes 40976
  798.0 106.6 %reduce-scatter.14.cloned.1.call-done = f32[24,1280]{1,0:T(8,128)} async-done(((f32[768,1280]{1,0:T(8,128)}), f32[24,1280]{1,0:T(8,128)}) %reduce-scatter.14.cloned.1.call-update) | async-done | bytes 122896 | tf_op jit(solution)/shard_map/reduce_scatter | solution.py:285
  904.6 153.8 %reduce-scatter.18.cloned.1.call-done = f32[40,1280]{1,0:T(8,128)} async-done(((f32[1280,1280]{1,0:T(8,128)}), f32[40,1280]{1,0:T(8,128)}) %reduce-scatter.18.cloned.1.call-update) | async-done | bytes 204816 | tf_op jit(solution)/shard_map/reduce_scatter | solution.py:289
  1058.4 155.6 %reduce-scatter.16.cloned.1.call-done = f32[40,1280]{1,0:T(8,128)} async-done(((f32[1280,1280]{1,0:T(8,128)}), f32[40,1280]{1,0:T(8,128)}) %reduce-scatter.16.cloned.1.call-update) | async-done | bytes 204816 | tf_op jit(solution)/shard_map/reduce_scatter | solution.py:286
  1214.0 154.8 %reduce-scatter.20.cloned.1.call-done = f32[40,1280]{1,0:T(8,128)} async-done(((f32[1280,1280]{1,0:T(8,128)}), f32[40,1280]{1,0:T(8,128)}) %reduce-scatter.20.cloned.1.call-update) | async-done | bytes 204816 | tf_op jit(solution)/shard_map/reduce_scatter | solution.py:290
  (607 shorter events, 161.4 us)
Async XLA Ops:
  7.2 282.3 %all-gather.5.cloned.1.call-start = ((), (), s32[]{:S(2)}) async-start(), calls=%async_computation.7 | async-start | bytes 2027520 | tf_op jit(solution)/shard_map/all_gather | solution.py:76
  7.9 323.3 %all-gather.7.cloned.1.call-start = ((), (), s32[]{:S(2)}) async-start(), calls=%async_computation.8 | async-start | bytes 3379200 | tf_op jit(solution)/shard_map/all_gather | solution.py:77
  8.7 330.3 %all-gather.9.cloned.1.call-start = ((), (), s32[]{:S(2)}) async-start(), calls=%async_computation.9 | async-start | bytes 3379200 | tf_op jit(solution)/shard_map/all_gather | solution.py:80
  9.4 346.7 %all-gather.11.cloned.1.call-start = ((), (), s32[]{:S(2)}) async-start(), calls=%async_computation.10 | async-start | bytes 3379200 | tf_op jit(solution)/shard_map/all_gather | solution.py:81
  10.0 573.4 %reduce-scatter.12.cloned.1.call-start = ((), (), s32[]{:S(2)}) async-start(), calls=%async_computation.12 | async-start | bytes 811008 | tf_op jit(solution)/shard_map/reduce_scatter | solution.py:284
  10.0 75.2 %copy-start.185 = (bf16[40]{0:T(256)(128)(2,1)S(1)}, bf16[40]{0:T(256)(128)(2,1)}, u32[]{:S(2)}) copy-start(bf16[40]{0:T(256)(128)(2,1)} %param.21) | copy-start | bytes 244
  10.0 75.5 %copy-start.186 = (bf16[40]{0:T(256)(128)(2,1)S(1)}, bf16[40]{0:T(256)(128)(2,1)}, u32[]{:S(2)}) copy-start(bf16[40]{0:T(256)(128)(2,1)} %param.22) | copy-start | bytes 244
  10.1 75.7 %copy-start.187 = (bf16[40]{0:T(256)(128)(2,1)S(1)}, bf16[40]{0:T(256)(128)(2,1)}, u32[]{:S(2)}) copy-start(bf16[40]{0:T(256)(128)(2,1)} %param.27) | copy-start | bytes 244
  10.1 76.0 %copy-start.188 = (bf16[40]{0:T(256)(128)(2,1)S(1)}, bf16[40]{0:T(256)(128)(2,1)}, u32[]{:S(2)}) copy-start(bf16[40]{0:T(256)(128)(2,1)} %param.28) | copy-start | bytes 244
  10.1 76.2 %copy-start.189 = (bf16[24]{0:T(256)(128)(2,1)S(1)}, bf16[24]{0:T(256)(128)(2,1)}, u32[]{:S(2)}) copy-start(bf16[24]{0:T(256)(128)(2,1)} %param.19) | copy-start | bytes 148
  10.1 76.4 %copy-start.190 = (bf16[24]{0:T(256)(128)(2,1)S(1)}, bf16[24]{0:T(256)(128)(2,1)}, u32[]{:S(2)}) copy-start(bf16[24]{0:T(256)(128)(2,1)} %param.20) | copy-start | bytes 148
  10.1 114.3 %copy-start.117 = (bf16[40,256]{1,0:T(8,128)(2,1)S(1)}, bf16[40,256]{1,0:T(8,128)(2,1)}, u32[]{:S(2)}) copy-start(bf16[40,256]{1,0:T(8,128)(2,1)} %param.23) | copy-start | bytes 61444
  84.9 184.9 %copy-start.88 = (f32[256]{0:T(256)}, f32[256]{0:T(256)S(1)}, u32[]{:S(2)}) copy-start(f32[256]{0:T(256)S(1)} %broadcast_multiply_fusion.6) | copy-start | bytes 3076
  85.2 184.6 %copy-start.91 = (f32[256]{0:T(256)}, f32[256]{0:T(256)S(1)}, u32[]{:S(2)}) copy-start(f32[256]{0:T(256)S(1)} %fusion.145) | copy-start | bytes 3076
  124.4 145.4 %copy-start.75 = (f32[1280]{0:T(1024)}, f32[1280]{0:T(1024)S(1)}, u32[]{:S(2)}) copy-start(f32[1280]{0:T(1024)S(1)} %convert_element_type.337) | copy-start | bytes 15364
  124.4 145.4 %copy-start.79 = (f32[1280]{0:T(1024)}, f32[1280]{0:T(1024)S(1)}, u32[]{:S(2)}) copy-start(f32[1280]{0:T(1024)S(1)} %convert_element_type.338) | copy-start | bytes 15364
  196.2 108.0 %copy-start.132 = (f32[768]{0:T(1024)}, f32[768]{0:T(1024)S(1)}, u32[]{:S(2)}) copy-start(f32[768]{0:T(1024)S(1)} %convert_element_type.333) | copy-start | bytes 9220
  199.5 89.9 %copy-start.100 = (f32[1024]{0:T(1024)}, f32[1024]{0:T(1024)S(1)}, u32[]{:S(2)}) copy-start(f32[1024]{0:T(1024)S(1)} %broadcast_multiply_fusion.2) | copy-start | bytes 12292
  199.5 97.3 %copy-start.106 = (f32[1024]{0:T(1024)}, f32[1024]{0:T(1024)S(1)}, u32[]{:S(2)}) copy-start(f32[1024]{0:T(1024)S(1)} %get-tuple-element.187) | copy-start | bytes 12292
  199.6 104.6 %copy-start.103 = (f32[1024]{0:T(1024)}, f32[1024]{0:T(1024)S(1)}, u32[]{:S(2)}) copy-start(f32[1024]{0:T(1024)S(1)} %get-tuple-element.186) | copy-start | bytes 12292
  202.1 80.7 %copy-start.98 = (f32[1024]{0:T(1024)}, f32[1024]{0:T(1024)S(1)}, u32[]{:S(2)}) copy-start(f32[1024]{0:T(1024)S(1)} %get-tuple-element.71) | copy-start | bytes 12292
  202.1 87.3 %copy-start.135 = (f32[1024]{0:T(1024)}, f32[1024]{0:T(1024)S(1)}, u32[]{:S(2)}) copy-start(f32[1024]{0:T(1024)S(1)} %fusion.142) | copy-start | bytes 12292
  202.2 102.0 %copy-start.173 = (f32[768]{0:T(1024)}, f32[768]{0:T(1024)S(1)}, u32[]{:S(2)}) copy-start(f32[768]{0:T(1024)S(1)} %convert_element_type.334) | copy-start | bytes 9220
  269.9 117.1 %copy-start.118 = (pred[1024]{0:T(1024)(128)(4,1)}, pred[1024]{0:T(1024)(128)(4,1)S(1)}, u32[]{:S(2)}) copy-start(pred[1024]{0:T(1024)(128)(4,1)S(1)} %iota_compare_fusion.2) | copy-start | bytes 3076
  276.2 110.7 %copy-start.81 = (f32[8,256]{1,0:T(8,128)}, f32[8,256]{1,0:T(8,128)S(1)}, u32[]{:S(2)}) copy-start(f32[8,256]{1,0:T(8,128)S(1)} %log_add_fusion.2) | copy-start | bytes 24580
  289.4 132.0 %copy-start.83 = (f32[8,256]{1,0:T(8,128)}, f32[8,256]{1,0:T(8,128)S(1)}, u32[]{:S(2)}) copy-start(f32[8,256]{1,0:T(8,128)S(1)} %log_add_fusion) | copy-start | bytes 24580
  430.8 231.8 %reduce-scatter.10.cloned.1.call-start = ((), (), s32[]{:S(2)}) async-start(), calls=%async_computation.11 | async-start | bytes 1351680 | tf_op jit(solution)/shard_map/reduce_scatter | solution.py:283
  440.5 357.5 %reduce-scatter.22.cloned.1.call-start = ((), (), s32[]{:S(2)}) async-start(), calls=%async_computation.17 | async-start | bytes 1351680
  462.9 441.7 %reduce-scatter.14.cloned.1.call-start = ((), (), s32[]{:S(2)}) async-start(), calls=%async_computation.13 | async-start | bytes 4055040 | tf_op jit(solution)/shard_map/reduce_scatter | solution.py:285
  479.8 578.6 %reduce-scatter.18.cloned.1.call-start = ((), (), s32[]{:S(2)}) async-start(), calls=%async_computation.15 | async-start | bytes 6758400 | tf_op jit(solution)/shard_map/reduce_scatter | solution.py:289
  487.9 726.1 %reduce-scatter.16.cloned.1.call-start = ((), (), s32[]{:S(2)}) async-start(), calls=%async_computation.14 | async-start | bytes 6758400 | tf_op jit(solution)/shard_map/reduce_scatter | solution.py:286
  495.3 873.5 %reduce-scatter.20.cloned.1.call-start = ((), (), s32[]{:S(2)}) async-start(), calls=%async_computation.16 | async-start | bytes 6758400 | tf_op jit(solution)/shard_map/reduce_scatter | solution.py:290
  (192 other events, 1503.1 us)
Sparse Core Ops, SparseCore 0:
  10.9 59.7 all-gather.4
  73.5 58.9 all-gather.6
  135.4 59.7 all-gather.8
  197.9 58.4 all-gather.10
  430.9 93.9 reduce-scatter.11
  527.6 134.9 reduce-scatter.9
  665.5 132.4 reduce-scatter.21
  804.0 100.5 reduce-scatter.13
  907.5 150.8 reduce-scatter.17
  1061.1 152.8 reduce-scatter.15
  1216.9 151.8 reduce-scatter.19
where the time goes:
time: 1380 us
  waiting for transfers between devices  788 us (57%)
  blocking collectives  289 us (21%)
  matrix products  187 us (14%)
  local copies, waits for them, and re-layouts  46.9 us (3%)
  other arithmetic  45.4 us (3%)
  between operations  17.2 us (1%)
    reduce_scatter x1, waiting for transfers between devices, per_device(): lax.psum_scatter(sum_output, ('dp', 'fsdp'), scatter_dimension=0, tiled=T...  156 us
    reduce_scatter x1, waiting for transfers between devices, per_device(): lax.psum_scatter(sum_down, ('dp', 'fsdp'), scatter_dimension=0, tiled=True)  155 us
    reduce_scatter x1, waiting for transfers between devices, per_device(): lax.psum_scatter(sum_up, ('dp', 'fsdp'), scatter_dimension=0, tiled=True)  154 us
    unnamed x12, waiting for transfers between devices  138 us
    reduce_scatter x1, waiting for transfers between devices, per_device(): lax.psum_scatter(sum_value, ('dp', 'fsdp'), scatter_dimension=0, tiled=True)  107 us
    reduce_scatter x1, waiting for transfers between devices, per_device(): lax.psum_scatter(sum_query, ('dp', 'fsdp'), scatter_dimension=0, tiled=True)  79.2 us
    unnamed x2, blocking collectives  76.8 us
    all_gather x1, blocking collectives, per_device(): lax.all_gather(latent_array, ('dp', 'fsdp'), axis=1, tiled=True)  74.3 us
  transfers between devices with their start and end apart: 11, of which 6 were waited for; matrix products, arithmetic and copies ran while one was open for 14% of the time, Pallas kernels for 0%

commit v1 on v0

--- a/solution.py
+++ b/solution.py
@@ -9,6 +9,29 @@
 HEADS = 8
 MB = 3
 epsilon = 1e-05
+
+
+def in_order(parts, dim):
+    parts = jnp.moveaxis(parts, 0, dim)
+    shape = parts.shape
+    return parts.reshape(*shape[:dim], shape[dim] * shape[dim + 1], *shape[dim + 2 :])
+
+
+def collected_by_bits(array, axis):
+    size, index = (lax.axis_size(axis), lax.axis_index(axis))
+    blocks, apart = (array[None], 1)
+    while apart < size:
+        received = lax.ppermute(blocks, axis, [(i, i ^ apart) for i in range(size)])
+        low = index & apart == 0
+        blocks = jnp.concatenate(
+            [jnp.where(low, blocks, received), jnp.where(low, received, blocks)]
+        )
+        apart *= 2
+    return blocks
+
+
+def doubled_up(shard, axis, dim):
+    return in_order(collected_by_bits(shard, axis), dim)
 
 
 def normalize(source, gain_vector, bias_vector):
@@ -72,7 +95,7 @@
             lax.all_gather(gain_latent, ("dp", "fsdp"), axis=0, tiled=True),
             lax.all_gather(bias_latent, ("dp", "fsdp"), axis=0, tiled=True),
             lax.all_gather(query_weight, ("dp", "fsdp"), axis=0, tiled=True),
-            lax.all_gather(key_weight, ("dp", "fsdp"), axis=0, tiled=True),
+            doubled_up(key_weight, ("dp", "fsdp"), 0),
             lax.all_gather(value_weight, ("dp", "fsdp"), axis=0, tiled=True),
             lax.all_gather(output_weight, ("dp", "fsdp"), axis=0, tiled=True),
             lax.all_gather(gain_feed, ("dp", "fsdp"), axis=0, tiled=True),

time: 1380 us -> 1340 us (0.971)
  waiting for transfers between devices: 788 us -> 731 us
    reduce_scatter x1, waiting for transfers between devices: 79.2 us -> 6.01 us  [per_device(): lax.psum_scatter(sum_query, ('dp', 'fsdp'), scatter_dimension=0, tiled=True)]
    ppermute x0 -> x5, waiting for transfers between devices: none -> 16.4 us  [collected_by_bits(): received = lax.ppermute(blocks, axis, [(i, i ^ apart) for i in range(size)])]
    unnamed x445 -> x401, local copies, waits for them, and re-layouts: 30.8 us -> 34.3 us
  transfers between devices with their start and end apart: 11 -> 16, of which waited for: 6 -> 10; matrix products, arithmetic and copies ran while one was open for 14% -> 15% of each run, Pallas kernels for 0% -> 0%
where the time goes in v1:
time: 1340 us; the launch traced here: 1330 us
  waiting for transfers between devices  731 us (55%)
  blocking collectives  286 us (21%)
  matrix products  193 us (14%)
  local copies, waits for them, and re-layouts  50.3 us (4%)
  other arithmetic  49.3 us (4%)
  between operations  16.9 us (1%)
    reduce_scatter x1, waiting for transfers between devices, per_device(): lax.psum_scatter(sum_down, ('dp', 'fsdp'), scatter_dimension=0, tiled=True)  156 us
    reduce_scatter x1, waiting for transfers between devices, per_device(): lax.psum_scatter(sum_up, ('dp', 'fsdp'), scatter_dimension=0, tiled=True)  155 us
    reduce_scatter x1, waiting for transfers between devices, per_device(): lax.psum_scatter(sum_output, ('dp', 'fsdp'), scatter_dimension=0, tiled=T...  154 us
    unnamed x12, waiting for transfers between devices  138 us
    reduce_scatter x1, waiting for transfers between devices, per_device(): lax.psum_scatter(sum_value, ('dp', 'fsdp'), scatter_dimension=0, tiled=True)  107 us
    unnamed x2, blocking collectives  78.9 us
    all_gather x1, blocking collectives, per_device(): lax.all_gather(latent_array, ('dp', 'fsdp'), axis=1, tiled=True)  70.9 us
    all_gather x1, blocking collectives, per_device(): lax.all_gather(query_weight, ('dp', 'fsdp'), axis=0, tiled=True)  69.1 us
  transfers between devices with their start and end apart: 16, of which 10 were waited for; matrix products, arithmetic and copies ran while one was open for 15% of the time, Pallas kernels for 0%

profile of v1, /device:TPU:0, one launch (start us, length us, event | category | flops | bytes accessed | tf_op | source)
XLA Modules:
  0.0 1333.0 jit_solution(6115344594657330313)
XLA Ops:
  17.6 40.0 %all-reduce.13 = (bf16[768]{0:T(1024)(128)(2,1)S(1)}, bf16[768]{0:T(1024)(128)(2,1)S(1)}, bf16[1280]{0:T(1024)(128)(2,1)S(1)}, bf16[1280]{0:T(1024)(128)(2,1)S(1...) all-reduce(bf16[768]{0:T(1024)(128)(2,1)S(1)} %dynamic-update-slice, ...), channel_id=1, replica_groups=mesh['dp'=4,'fsdp'=8] {'dp','fsdp'}, use_global_device_ids=true, to_apply=%add.1 | all-reduce | flops 6656 | bytes 26624
  64.0 70.9 %all_gather.26 = bf16[256,1280]{0,1:T(8,128)(2,1)S(1)} all-gather(bf16[256,40]{0,1:T(8,128)(2,1)S(1)} %copy-done.116), channel_id=1, replica_groups=mesh['dp'=4,'fsdp'=8] {'dp','fsdp'}, dimensions={1}, use_global_device_ids=true | all-gather | bytes 675840 | tf_op jit(solution)/shard_map/all_gather | solution.py:92
  135.6 69.1 %all_gather.32 = bf16[1280,256]{1,0:T(8,128)(2,1)S(1)} all-gather(bf16[40,256]{1,0:T(8,128)(2,1)S(1)} %copy-done.117), channel_id=1, replica_groups=mesh['dp'=4,'fsdp'=8] {'dp','fsdp'}, dimensions={0}, use_global_device_ids=true | all-gather | bytes 675840 | tf_op jit(solution)/shard_map/all_gather | solution.py:97
  213.3 4.5 collective-permute-done.2
  221.3 8.1 collective-permute-done.4
  246.6 4.5 convolution_convert_fusion.2
  254.1 4.5 convolution_convert_fusion.1
  261.4 6.0 convolution_convert_fusion
  270.4 8.1 convolution_convert_fusion.11
  278.5 6.5 convolution_convert_fusion.10
  296.3 7.0 multiply_convert_fusion.5
  303.3 4.9 multiply_convert_fusion.4
  308.2 5.1 multiply_convert_fusion.3
  337.4 6.8 multiply_reduce_fusion.2
  354.7 6.8 multiply_reduce_fusion.1
  372.0 6.8 multiply_reduce_fusion
  400.9 5.3 add_add_fusion.10
  409.1 7.1 convolution_convert_fusion.8
  416.2 7.1 convolution_convert_fusion.7
  428.0 4.2 fusion.191
  436.2 6.0 add_add_fusion.3
  467.3 67.5 %all_gather.38 = bf16[768,256]{1,0:T(8,128)(2,1)S(1)} all-gather(bf16[24,256]{1,0:T(8,128)(2,1)S(1)} %copy-done.91), channel_id=1, replica_groups=mesh['dp'=4,'fsdp'=8] {'dp','fsdp'}, dimensions={0}, use_global_device_ids=true | all-gather | bytes 405504 | tf_op jit(solution)/shard_map/all_gather | solution.py:186
  534.8 4.6 fusion.214
  548.3 7.0 fusion.47
  555.4 38.9 %all-reduce.12 = (f32[768]{0:T(1024)S(1)}, f32[768]{0:T(1024)S(1)}, f32[1280]{0:T(1024)S(1)}, f32[1280]{0:T(1024)S(1)}, f32[1280]{0:T(1024)S(1)}, /*index=5*/f32[1280]{0:T(1024)S(1)}) all-reduce(f32[768]{0:T(1024)S(1)} %add_add_fusion.19, f32[768]{0:T(1024)S(1)} %add_add_fusion.18, ...), channel_id=3, replica_groups=mesh['dp'=4,'fsdp'=8] {'dp','fsdp'}, use_global_device_ids=true, to_apply=%region_45.46.clone | all-reduce | flops 6656 | bytes 53248
  597.9 7.5 fusion.201
  614.2 6.0 reduce-scatter.10.cloned.1.call-done
  620.2 135.7 %reduce-scatter.22.cloned.1.call-done = f32[40,256]{1,0:T(8,128)} async-done(((f32[1280,256]{1,0:T(8,128)}), f32[40,256]{1,0:T(8,128)}) %reduce-scatter.22.cloned.1.call-update) | async-done | bytes 40976
  755.9 106.5 %reduce-scatter.14.cloned.1.call-done = f32[24,1280]{1,0:T(8,128)} async-done(((f32[768,1280]{1,0:T(8,128)}), f32[24,1280]{1,0:T(8,128)}) %reduce-scatter.14.cloned.1.call-update) | async-done | bytes 122896 | tf_op jit(solution)/shard_map/reduce_scatter | solution.py:308
  862.5 154.5 %reduce-scatter.18.cloned.1.call-done = f32[40,1280]{1,0:T(8,128)} async-done(((f32[1280,1280]{1,0:T(8,128)}), f32[40,1280]{1,0:T(8,128)}) %reduce-scatter.18.cloned.1.call-update) | async-done | bytes 204816 | tf_op jit(solution)/shard_map/reduce_scatter | solution.py:312
  1017.0 153.6 %reduce-scatter.16.cloned.1.call-done = f32[40,1280]{1,0:T(8,128)} async-done(((f32[1280,1280]{1,0:T(8,128)}), f32[40,1280]{1,0:T(8,128)}) %reduce-scatter.16.cloned.1.call-update) | async-done | bytes 204816 | tf_op jit(solution)/shard_map/reduce_scatter | solution.py:309
  1170.6 155.7 %reduce-scatter.20.cloned.1.call-done = f32[40,1280]{1,0:T(8,128)} async-done(((f32[1280,1280]{1,0:T(8,128)}), f32[40,1280]{1,0:T(8,128)}) %reduce-scatter.20.cloned.1.call-update) | async-done | bytes 204816 | tf_op jit(solution)/shard_map/reduce_scatter | solution.py:313
  (584 shorter events, 189.3 us)
Async XLA Ops:
  7.2 239.4 %all-gather.5.cloned.1.call-start = ((), (), s32[]{:S(2)}) async-start(), calls=%async_computation.7 | async-start | bytes 2027520 | tf_op jit(solution)/shard_map/all_gather | solution.py:99
  7.9 280.6 %all-gather.7.cloned.1.call-start = ((), (), s32[]{:S(2)}) async-start(), calls=%async_computation.8 | async-start | bytes 3379200 | tf_op jit(solution)/shard_map/all_gather | solution.py:100
  8.7 287.6 %all-gather.9.cloned.1.call-start = ((), (), s32[]{:S(2)}) async-start(), calls=%async_computation.9 | async-start | bytes 3379200 | tf_op jit(solution)/shard_map/all_gather | solution.py:103
  9.4 304.0 %all-gather.11.cloned.1.call-start = ((), (), s32[]{:S(2)}) async-start(), calls=%async_computation.10 | async-start | bytes 3379200 | tf_op jit(solution)/shard_map/all_gather | solution.py:104
  9.4 199.0 %collective-permute-start = (bf16[1,24,256]{2,1,0:T(8,128)(2,1)}, bf16[1,24,256]{2,1,0:T(8,128)(2,1)S(1)}, u32[]{:S(2)}, u32[]{:S(2)}) collective-permute-start(bf16[1,24,256]{2,1,0:T(8,128)(2,1)} %bitcast.373), channel_id=1, source_target_pairs={{0,1},{1,0},{2,3},{3,2},{4,5},{5,4},{6,7},{7,6},{8,9},{9,8},{10,11... | collective-permute-start | bytes 36872 | tf_op jit(solution)/shard_map/ppermute | solution.py:24
  12.5 601.7 %reduce-scatter.12.cloned.1.call-start = ((), (), s32[]{:S(2)}) async-start(), calls=%async_computation.12 | async-start | bytes 811008 | tf_op jit(solution)/shard_map/reduce_scatter | solution.py:307
  57.7 328.8 %copy-start.100 = (f32[768]{0:T(1024)}, f32[768]{0:T(1024)S(1)}, u32[]{:S(2)}) copy-start(f32[768]{0:T(1024)S(1)} %convert_element_type.339) | copy-start | bytes 9220
  57.7 183.1 %copy-start.118 = (f32[768]{0:T(1024)}, f32[768]{0:T(1024)S(1)}, u32[]{:S(2)}) copy-start(f32[768]{0:T(1024)S(1)} %convert_element_type.340) | copy-start | bytes 9220
  60.9 185.7 %copy-start.88 = (f32[1024]{0:T(1024)}, f32[1024]{0:T(1024)S(1)}, u32[]{:S(2)}) copy-start(f32[1024]{0:T(1024)S(1)} %broadcast_multiply_fusion.2) | copy-start | bytes 12292
  61.0 324.0 %copy-start.106 = (f32[1024]{0:T(1024)}, f32[1024]{0:T(1024)S(1)}, u32[]{:S(2)}) copy-start(f32[1024]{0:T(1024)S(1)} %get-tuple-element.197) | copy-start | bytes 12292
  61.0 325.5 %copy-start.104 = (f32[1024]{0:T(1024)}, f32[1024]{0:T(1024)S(1)}, u32[]{:S(2)}) copy-start(f32[1024]{0:T(1024)S(1)} %get-tuple-element.196) | copy-start | bytes 12292
  63.4 141.4 %copy-start.96 = (f32[1024]{0:T(1024)}, f32[1024]{0:T(1024)S(1)}, u32[]{:S(2)}) copy-start(f32[1024]{0:T(1024)S(1)} %get-tuple-element.72) | copy-start | bytes 12292
  63.4 157.9 %copy-start.98 = (f32[1024]{0:T(1024)}, f32[1024]{0:T(1024)S(1)}, u32[]{:S(2)}) copy-start(f32[1024]{0:T(1024)S(1)} %get-tuple-element.71) | copy-start | bytes 12292
  63.4 183.2 %copy-start.102 = (f32[1024]{0:T(1024)}, f32[1024]{0:T(1024)S(1)}, u32[]{:S(2)}) copy-start(f32[1024]{0:T(1024)S(1)} %fusion.160) | copy-start | bytes 12292
  63.5 143.7 %copy-start.74 = (f32[1280]{0:T(1024)}, f32[1280]{0:T(1024)S(1)}, u32[]{:S(2)}) copy-start(f32[1280]{0:T(1024)S(1)} %convert_element_type.343) | copy-start | bytes 15364
  64.0 143.1 %copy-start.76 = (f32[1280]{0:T(1024)}, f32[1280]{0:T(1024)S(1)}, u32[]{:S(2)}) copy-start(f32[1280]{0:T(1024)S(1)} %convert_element_type.344) | copy-start | bytes 15364
  135.3 71.9 %copy-start.86 = (f32[256]{0:T(256)}, f32[256]{0:T(256)S(1)}, u32[]{:S(2)}) copy-start(f32[256]{0:T(256)S(1)} %broadcast_multiply_fusion.6) | copy-start | bytes 3076
  208.5 4.0 collective-permute-start.1
  212.5 5.2 collective-permute-start.2
  213.3 95.0 %copy-start.78 = (f32[1280]{0:T(1024)}, f32[1280]{0:T(1024)S(1)}, u32[]{:S(2)}) copy-start(f32[1280]{0:T(1024)S(1)} %convert_element_type.355) | copy-start | bytes 15364
  217.8 1.4 collective-permute-start.3
  219.2 10.2 collective-permute-start.4
  221.3 165.2 %copy-start.139 = (f32[1024]{0:T(1024)}, f32[1024]{0:T(1024)S(1)}, u32[]{:S(2)}) copy-start(f32[1024]{0:T(1024)S(1)} %fusion.162) | copy-start | bytes 12292
  235.0 109.3 %copy-start.82 = (f32[8,256]{1,0:T(8,128)}, f32[8,256]{1,0:T(8,128)S(1)}, u32[]{:S(2)}) copy-start(f32[8,256]{1,0:T(8,128)S(1)} %log_add_fusion.2) | copy-start | bytes 24580
  240.8 120.7 %copy-start.84 = (f32[8,256]{1,0:T(8,128)}, f32[8,256]{1,0:T(8,128)S(1)}, u32[]{:S(2)}) copy-start(f32[8,256]{1,0:T(8,128)S(1)} %log_add_fusion.1) | copy-start | bytes 24580
  246.6 132.2 %copy-start.80 = (f32[8,256]{1,0:T(8,128)}, f32[8,256]{1,0:T(8,128)S(1)}, u32[]{:S(2)}) copy-start(f32[8,256]{1,0:T(8,128)S(1)} %log_add_fusion) | copy-start | bytes 24580
  388.6 231.6 %reduce-scatter.10.cloned.1.call-start = ((), (), s32[]{:S(2)}) async-start(), calls=%async_computation.11 | async-start | bytes 1351680 | tf_op jit(solution)/shard_map/reduce_scatter | solution.py:306
  399.5 356.4 %reduce-scatter.22.cloned.1.call-start = ((), (), s32[]{:S(2)}) async-start(), calls=%async_computation.17 | async-start | bytes 1351680
  423.4 439.0 %reduce-scatter.14.cloned.1.call-start = ((), (), s32[]{:S(2)}) async-start(), calls=%async_computation.13 | async-start | bytes 4055040 | tf_op jit(solution)/shard_map/reduce_scatter | solution.py:308
  442.2 574.8 %reduce-scatter.18.cloned.1.call-start = ((), (), s32[]{:S(2)}) async-start(), calls=%async_computation.15 | async-start | bytes 6758400 | tf_op jit(solution)/shard_map/reduce_scatter | solution.py:312
  450.3 720.3 %reduce-scatter.16.cloned.1.call-start = ((), (), s32[]{:S(2)}) async-start(), calls=%async_computation.14 | async-start | bytes 6758400 | tf_op jit(solution)/shard_map/reduce_scatter | solution.py:309
  457.9 868.4 %reduce-scatter.20.cloned.1.call-start = ((), (), s32[]{:S(2)}) async-start(), calls=%async_computation.16 | async-start | bytes 6758400 | tf_op jit(solution)/shard_map/reduce_scatter | solution.py:313
  (175 other events, 1240.0 us)
Sparse Core Ops, SparseCore 0:
  10.9 58.9 all-gather.4
  72.8 59.8 all-gather.6
  135.5 59.2 all-gather.8
  197.5 58.5 all-gather.10
  388.7 93.9 reduce-scatter.11
  485.4 134.7 reduce-scatter.9
  623.1 132.7 reduce-scatter.21
  761.9 100.5 reduce-scatter.13
  865.3 151.6 reduce-scatter.17
  1019.7 150.8 reduce-scatter.15
  1173.5 152.7 reduce-scatter.19
